TPU v7x, 32 devices: a whole 2x2x4 slice. The times are simulated.
32 devices in a mesh: group: 4 (over y, x), tile: 4 (over z), video: 2 (over core).
Axes of the slice: x: 2, y: 2, z: 4, core: 2. Of those that a mesh axis runs over, the one named last changes fastest.
Arguments:
- features: bfloat16 [8, 8, 16, 24, 384], P(('video', 'tile'), 'group'), parts along dimension 0, may hold values from -6 to 6
- group_slot: int32 [4], replicated, may hold values from 0 to 3, each once
- margins: int32 [4, 4], P('tile'), may hold values from 0 to 4, as said below
- norm_gain: float32 [384], replicated, may hold values from 0.1 to 1.9
- kernel: bfloat16 [3, 3, 3, 384, 384], replicated, may hold values from -0.0625 to 0.0625
- conv_bias: float32 [384], replicated, may hold values from -3 to 3
Outputs:
- decoded: bfloat16 [8, 8, 16, 24, 384], P(('video', 'tile'), 'group'), parts along dimension 0
There are 2 independent parts, one for each index of `video`. A program takes and returns all parts, laid end to end along the dimension named above; an argument that names none is the same for every part. Nothing has to cross between parts.
Inputs may be any that keep to these rules, and one draw needn't show every extreme that they name: group_slot is a permutation of 0 to 3. margins[t] is (left, right, up, down) of tile t; a margin is 0 exactly at the image's border and 1 to 4 elsewhere; the margin a tile has toward a neighbour equals the neighbour's margin back; left and right margins depend only on the tile's column, up and down margins are the same for all columns; some margin equals 4.
All inputs are finite; a program needn't handle non-finite values.
Results may differ from a plain program's by a relative error of at most 0.0043.
Values may be sent and summed in bfloat16 or wider, within the bound.
A program may use at most 128 MiB of HBM per device.

v0:
```python
import functools

import jax
import jax.numpy as jnp
from jax import lax
from jax.experimental import pallas as pl
from jax.experimental.pallas import tpu as pltpu
from jax.sharding import PartitionSpec as P

GRID_R = 2
M = 4
MESH = pl.DeviceIdType.MESH
DIRS = ((-1, 0), (1, 0), (0, -1), (0, 1), (-1, -1), (-1, 1), (1, -1), (1, 1))


def activate(values, gain):
    widened = values.astype(jnp.float32)
    inv_norm = lax.rsqrt(jnp.mean(widened * widened, axis=-1, keepdims=True) + 1e-06)
    half = widened * inv_norm * (0.5 * gain)
    return half + half * jnp.tanh(half)


def body(n_group, n_tile, slot_ref, margin_ref, x_hbm, gain_ref, bias_ref, w_hbm, out_ref,
         x_ref, first_in, second_in, relay, rows_in, cols_in, corners_in, cols_out, w, act, z, edge, acc,
         send_small, recv_small, send_big, recv_big, w_sem, x_sem):
    frames, core_h, core_w, channels = x_ref.shape
    grid_cols = n_tile // GRID_R
    lanes = channels // 128
    pitch = core_w + 16
    half = core_h // 2
    cut = core_w - 8
    pieces = ((0, cut), (cut, core_w))
    group = lax.axis_index("group")
    tile = lax.axis_index("tile")
    tile_row = tile // grid_cols
    tile_col = tile % grid_cols
    partners = (group + 1 - 2 * (group % 2), (group + n_group // 2) % n_group)

    def present(step_r, step_c):
        ok = None
        for at, step, most in ((tile_row, step_r, GRID_R), (tile_col, step_c, grid_cols)):
            if step == 0:
                continue
            here = (at > 0) if step < 0 else (at < most - 1)
            ok = here if ok is None else jnp.logical_and(ok, here)
        return ok

    barrier = pltpu.get_barrier_semaphore()
    greeted = jnp.int32(2)
    for peer in partners:
        pl.semaphore_signal(barrier, inc=1, device_id={"group": peer}, device_id_type=MESH)
    for step_r, step_c in DIRS:
        ok = present(step_r, step_c)
        greeted = greeted + ok.astype(jnp.int32)

        @pl.when(ok)
        def _():
            pl.semaphore_signal(barrier, inc=1, device_id={"tile": tile + step_r * grid_cols + step_c},
                                device_id_type=MESH)

    x_copy = pltpu.make_async_copy(x_hbm, x_ref, x_sem)
    x_copy.start()

    def w_copy(a):
        return pltpu.make_async_copy(w_hbm.at[a], w.at[:, pl.ds((2 - a) * channels, channels)], w_sem.at[a])

    for a in (2, 1, 0):
        w_copy(a).start()

    def rim_at(stage, n):
        step_r, step_c = DIRS[n]
        if step_c == 0:
            return rows_in.at[stage, 1 if step_r > 0 else 0]
        if step_r == 0:
            return cols_in.at[stage, 1 if step_c > 0 else 0]
        return corners_in.at[stage, 1 if step_r > 0 else 0, 1 if step_c > 0 else 0]

    def rim_copy(n):
        step_r, step_c = DIRS[n]
        row = 0 if step_r < 0 else core_h - 1
        if step_c == 0:
            src = x_hbm.at[:, row]
        elif step_r == 0:
            src = cols_out.at[0 if step_c < 0 else 1]
        else:
            src = x_hbm.at[:, row, pl.ds(0 if step_c < 0 else core_w - 8, 8)]
        return pltpu.make_async_remote_copy(
            src_ref=src, dst_ref=rim_at(0, DIRS.index((-step_r, -step_c))),
            send_sem=send_small.at[0, n], recv_sem=recv_small.at[0, n],
            device_id={"tile": tile + step_r * grid_cols + step_c}, device_id_type=MESH)

    def way(n):
        return 0 if DIRS[n][1] == 0 else 1

    def rim_pass(phase, n):
        return pltpu.make_async_remote_copy(
            src_ref=rim_at(0 if phase == 1 else 3, n), dst_ref=rim_at(phase, n),
            send_sem=send_small.at[phase, n], recv_sem=recv_small.at[phase, n],
            device_id={"group": partners[way(n) if phase == 1 else 1 - way(n)]}, device_id_type=MESH)

    def block_pass(phase, f, k, h):
        cols = pl.ds(pieces[k][0], pieces[k][1] - pieces[k][0])
        rows = pl.ds(h * half, half)
        return pltpu.make_async_remote_copy(
            src_ref=(x_hbm if phase == 1 else relay).at[f, rows, cols],
            dst_ref=(first_in if phase == 1 else second_in).at[f, rows, cols],
            send_sem=send_big.at[phase - 1, f, 2 * k + h], recv_sem=recv_big.at[phase - 1, f, 2 * k + h],
            device_id={"group": partners[h if phase == 1 else 1 - h]}, device_id_type=MESH)

    def for_dirs(act_on, side=None):
        for n, (step_r, step_c) in enumerate(DIRS):
            if side is None or (step_r == 0) == side:
                pl.when(present(step_r, step_c))(functools.partial(act_on, n))

    def opposite(n):
        return DIRS.index((-DIRS[n][0], -DIRS[n][1]))

    pl.semaphore_wait(barrier, greeted)
    for_dirs(lambda n: rim_copy(n).start(), False)
    for k in (0, 1):
        for h in (0, 1):
            block_pass(1, 1, k, h).start()

    zero_rim = jnp.zeros((pitch, 128), jnp.float32)
    for slot in range(2):
        for c in range(lanes):
            act[slot, c, pl.ds(0, pitch)] = zero_rim
            act[slot, c, pl.ds((core_h + 1) * pitch, pitch)] = zero_rim
            act[slot, c, pl.ds(pitch + 7, core_h, stride=pitch)] = zero_rim[:core_h]
            act[slot, c, pl.ds(pitch + 8 + core_w, core_h, stride=pitch)] = zero_rim[:core_h]

    x_copy.wait()
    for f in range(frames):
        side = x_ref[f].astype(jnp.float32)
        cols_out[0, f] = side[:, 0, :].astype(jnp.bfloat16)
        cols_out[1, f] = side[:, core_w - 1, :].astype(jnp.bfloat16)
    for_dirs(lambda n: rim_copy(n).start(), True)

    gain = gain_ref[...].reshape(1, channels)
    left, right, up, down = [margin_ref[0, k] for k in range(4)]
    place = slot_ref[group]
    places = [slot_ref[p] for p in partners]
    mine = [jnp.full((1, channels), places[h] == place - 1) for h in (0, 1)]
    theirs = [jnp.full((1, channels), places[h] == places[1 - h] - 1) for h in (0, 1)]

    def choose(hit, a, b):
        return jnp.where(hit, a.astype(jnp.float32), b.astype(jnp.float32))

    not_first = jnp.where(jnp.full((core_h, channels), place > 0), 1.0, 0.0)

    def kept(m):
        m_f = jnp.full((core_h, channels), m, jnp.int32).astype(jnp.float32)
        return (m_f + 1.0) / (m_f + 2.0)

    row_at = lax.broadcasted_iota(jnp.int32, (core_h, channels), 0)
    alpha = [jnp.where(row_at == core_h - down, kept(down), 1.0), None,
             jnp.where(row_at == up - 1, kept(up), 1.0)]
    beta_left = kept(left)
    beta_right = kept(right)

    def put_act(slot, at, v):
        for c in range(lanes):
            act[slot, c, at] = v[:, c * 128:(c + 1) * 128]

    def interior(kind, f, slot, first, last):
        def some_rows(i, carry):
            for h in (0, 1):
                for k in range(2):
                    row = h * half + 2 * i + k
                    if kind:
                        v = choose(mine[h], first_in[f, row, first:last], second_in[f, row, first:last])
                    else:
                        v = x_ref[f, row, first:last]
                    at = pl.multiple_of((row + 1) * pitch + 8 + first, 8)
                    put_act(slot, pl.ds(at, last - first), activate(v, gain))
            return carry
        lax.fori_loop(0, half // 2, some_rows, 0)

    def forward(f, k):
        first, last = pieces[k]
        for h in (0, 1):
            block_pass(1, f, k, h).wait_recv()

        def some_rows(i, carry):
            for h in (0, 1):
                row = h * half + i
                relay[f, row, first:last] = choose(theirs[h], first_in[f, row, first:last],
                                                   x_ref[f, row, first:last]).astype(jnp.bfloat16)
            return carry
        lax.fori_loop(0, half, some_rows, 0, unroll=2)
        for h in (0, 1):
            block_pass(2, f, k, h).start()

    def forward_rim(n):
        rim_pass(1, n).wait_recv()
        hit = theirs[way(n)]
        for f in range(frames):
            rim_at(3, n)[f] = choose(hit, rim_at(1, n)[f], rim_at(0, n)[f]).astype(jnp.bfloat16)
        rim_pass(2, n).start()

    def rims(kind, f, slot):
        store = functools.partial(put_act, slot)

        def one(n):
            step_r, step_c = DIRS[n]
            if kind:
                v = choose(mine[way(n)], rim_at(1, n)[f], rim_at(2, n)[f])
            else:
                v = rim_at(0, n)[f]
            v = activate(v, gain)
            vertical = (core_h + 1) * pitch if step_r > 0 else 0
            if step_c == 0:
                store(pl.ds(vertical + 8, core_w), v)
            elif step_r == 0:
                store(pl.ds(pitch + (8 + core_w if step_c > 0 else 7), core_h, stride=pitch), v)
            else:
                store(pl.ds(vertical + (8 + core_w if step_c > 0 else 7), 1), v[0:1] if step_c > 0 else v[7:8])
        for_dirs(one)

    def column(kind, slot, b, p):
        at = pl.ds(b * pitch + 7 + p, core_h, stride=pitch)
        v = jnp.concatenate([act[slot, c, at] for c in range(lanes)], axis=-1)
        if alpha[b] is not None:
            v = v * alpha[b]
        return v * not_first if kind else v

    def spread(kind, slot, first, last):
        def one_col(p, carry):
            for b in range(3):
                z[slot, b, pl.ds(pl.multiple_of(p * core_h, core_h), core_h)] = column(kind, slot, b, p).astype(jnp.bfloat16)
            return carry
        lax.fori_loop(first, last, one_col, 0, unroll=2)

    def spread_left(kind, slot):
        for j in range(M):
            for b in range(3):
                v = column(kind, slot, b, j + 2)
                edge[slot, b, 1, j * core_h:(j + 1) * core_h] = jnp.where(j == left - 1, v * beta_left, v).astype(jnp.bfloat16)

    def spread_right(kind, slot):
        for j in range(M):
            for b in range(3):
                v = column(kind, slot, b, core_w - M + j)
                edge[slot, b, 0, j * core_h:(j + 1) * core_h] = jnp.where(M - j == right, v * beta_right, v).astype(jnp.bfloat16)

    def spread_all(kind, slot):
        spread(kind, slot, 0, core_w + 2)
        spread_left(kind, slot)
        spread_right(kind, slot)

    def windows(slot, j0, j1):
        def rows(ref, first, last):
            return ref[first * core_h:last * core_h]
        out = []
        for b in range(3):
            plain = z.at[slot, b]
            inner = min(j1, core_w - M)
            near = [rows(plain, j0, inner)]
            if j1 > inner:
                near.append(rows(edge.at[slot, b, 0], 0, j1 - inner))
            outer = max(j0, M)
            far = [rows(edge.at[slot, b, 1], j0, M)] if j0 < M else []
            far.append(rows(plain, outer + 2, j1 + 2))
            out += [jnp.concatenate(near, axis=0), rows(plain, j0 + 1, j1 + 1), jnp.concatenate(far, axis=0)]
        return jnp.concatenate(out, axis=-1)

    def multiply(slot, tap, target, many, j0, j1, between=None):
        at = slice(j0 * core_h, j1 * core_h)
        steps = many * lanes // 2 if many > 1 else lanes - 1
        stride = 2 if many > 1 else 1

        def step(n, carry):
            first = pl.multiple_of((tap * lanes + stride * n) * 128, 128)
            r = jnp.dot(windows(slot, j0, j1), w[:, pl.ds(first, 256)], preferred_element_type=jnp.float32)
            c = target * lanes + stride * n
            if many > 1:
                acc[c, at] += r[:, :128]
            else:
                @pl.when(n == 0)
                def _():
                    acc[c, at] += r[:, :128]
            acc[c + 1, at] += r[:, 128:]
            if between is not None:
                pl.when(n == 0)(between)
            return carry
        lax.fori_loop(0, steps, step, 0)

    bias = bias_ref[...].reshape(1, channels)

    def give(s, first, last):
        def put(i, carry):
            v = jnp.concatenate([acc[s * lanes + c, pl.ds(i + first * core_h, last - first, stride=core_h)]
                                 for c in range(lanes)], axis=-1)
            out_ref[s, i, first:last] = (v + bias).astype(out_ref.dtype)
            return carry
        lax.fori_loop(0, core_h, put, 0, unroll=4)

    def clear(i, carry):
        acc[i] = jnp.zeros(acc.shape[1:], jnp.float32)
        return carry
    lax.fori_loop(0, 2 * lanes, clear, 0)

    interior(0, 0, 0, 0, core_w)
    interior(0, 1, 1, 0, core_w)
    for_dirs(lambda n: rim_copy(opposite(n)).wait_recv())
    for_dirs(lambda n: rim_pass(1, n).start())
    for f in (0, 1):
        rims(0, f, f)
        spread_all(0, f)
        forward(1, f)
    for_dirs(forward_rim)
    for k in (0, 1):
        for h in (0, 1):
            block_pass(1, 0, k, h).start()
    w_copy(2).wait()
    w_copy(1).wait()
    multiply(0, 0, 0, 2, 0, core_w)
    multiply(1, 0, 1, 1, 0, core_w)

    for k in (0, 1):
        for h in (0, 1):
            block_pass(2, 1, k, h).wait_recv()
    interior(1, 1, 1, 0, core_w)
    for_dirs(lambda n: rim_pass(2, n).wait_recv())
    rims(1, 1, 1)
    spread_all(1, 1)
    forward(0, 0)
    w_copy(0).wait()
    multiply(1, 1, 0, 2, 0, core_w, functools.partial(forward, 0, 1))
    give(1, 0, core_w)

    for h in (0, 1):
        block_pass(2, 0, 0, h).wait_recv()
    interior(1, 0, 0, 0, cut)
    rims(1, 0, 0)
    spread(1, 0, 0, cut + 1)
    spread_left(1, 0)
    multiply(0, 2, 0, 1, 0, cut - 1)
    give(0, 0, cut - 8)
    for h in (0, 1):
        block_pass(2, 0, 1, h).wait_recv()
    interior(1, 0, 0, cut, core_w)
    spread(1, 0, cut + 1, core_w + 2)
    spread_right(1, 0)
    multiply(0, 2, 0, 1, cut - 1, core_w)
    give(0, cut - 8, core_w)

    def sent(n):
        rim_copy(n).wait_send()
        for phase in (1, 2):
            rim_pass(phase, n).wait_send()
    for_dirs(sent)
    for phase in (1, 2):
        for f in (1, 0):
            for k in (0, 1):
                for h in (0, 1):
                    block_pass(phase, f, k, h).wait_send()


def local(n_group, n_tile, features, group_slot, margins, norm_gain, kernel, conv_bias):
    x = features[0]
    frames, core_h, core_w, channels = x.shape
    weights = kernel.reshape(3, 9 * channels, channels)
    pitch = core_w + 16
    block = pltpu.VMEM((frames, core_h, core_w, channels), jnp.bfloat16)
    vmem = pl.BlockSpec(memory_space=pltpu.VMEM)
    smem = pl.BlockSpec(memory_space=pltpu.SMEM)
    anywhere = pl.BlockSpec(memory_space=pl.ANY)
    out = pl.pallas_call(
        functools.partial(body, n_group, n_tile),
        out_shape=jax.ShapeDtypeStruct(x.shape, jnp.bfloat16),
        in_specs=[smem, smem, anywhere, vmem, vmem, anywhere],
        out_specs=vmem,
        scratch_shapes=[
            block, block, block, block,
            pltpu.VMEM((4, 2, frames, core_w, channels), jnp.bfloat16),
            pltpu.VMEM((4, 2, frames, core_h, channels), jnp.bfloat16),
            pltpu.VMEM((4, 2, 2, frames, 8, channels), jnp.bfloat16),
            pltpu.VMEM((2, frames, core_h, channels), jnp.bfloat16),
            pltpu.VMEM((9 * channels, 3 * channels), jnp.bfloat16),
            pltpu.VMEM((2, channels // 128, (core_h + 2) * pitch, 128), jnp.float32),
            pltpu.VMEM((2, 3, (core_w + 2) * core_h, channels), jnp.bfloat16),
            pltpu.VMEM((2, 3, 2, M * core_h, channels), jnp.bfloat16),
            pltpu.VMEM((2 * channels // 128, core_h * core_w, 128), jnp.float32),
            pltpu.SemaphoreType.DMA((3, 8)),
            pltpu.SemaphoreType.DMA((3, 8)),
            pltpu.SemaphoreType.DMA((2, 2, 4)),
            pltpu.SemaphoreType.DMA((2, 2, 4)),
            pltpu.SemaphoreType.DMA((3,)),
            pltpu.SemaphoreType.DMA,
        ],
        compiler_params=pltpu.CompilerParams(collective_id=0, has_side_effects=True, vmem_limit_bytes=40 << 20),
        name="conv",
    )(group_slot, margins, x, norm_gain, conv_bias, weights)
    return out[None]


def solution(mesh):
    n_group = mesh.shape["group"]
    n_tile = mesh.shape["tile"]
    if n_group != 4:
        raise ValueError("group size")
    return jax.shard_map(
        functools.partial(local, n_group, n_tile),
        mesh=mesh,
        in_specs=(
            P(("video", "tile"), "group", None, None, None),
            P(),
            P("tile", None),
            P(),
            P(),
            P(),
        ),
        out_specs=P(("video", "tile"), "group", None, None, None),
        check_vma=False,
    )
```

profile of v0, /device:TPU:0, one launch (start us, length us, event | category | flops | bytes accessed | tf_op | source)
XLA Modules:
  0.0 35.7 jit_solution(14986796659967834412)
XLA Ops:
  0.0 0.0 copy-start
  0.0 3.3 %copy-done = bf16[3,3,3,384,384]{4,3,2,1,0:T(8,128)(2,1)S(1)} copy-done((bf16[3,3,3,384,384]{4,3,2,1,0:T(8,128)(2,1)S(1)}, bf16[3,3,3,384,384]{4,3,2,1,0:T(8,128)(2,1)}, u32[]{:S(2)}) %copy-start) | copy-done | bytes 7962648
  3.3 0.0 copy-start.1
  3.3 1.1 %copy-done.1 = bf16[1,2,16,24,384]{4,3,2,1,0:T(8,128)(2,1)S(1)} copy-done((bf16[1,2,16,24,384]{4,3,2,1,0:T(8,128)(2,1)S(1)}, bf16[1,2,16,24,384]{4,3,2,1,0:T(8,128)(2,1)}, u32[]{:S(2)}) %copy-start.1) | copy-done | bytes 589848
  4.3 0.0 copy-start.2
  4.3 0.7 %copy-done.2 = f32[384]{0:T(512)S(1)} copy-done((f32[384]{0:T(512)S(1)}, f32[384]{0:T(512)}, u32[]{:S(2)}) %copy-start.2) | copy-done | bytes 1560
  5.0 0.0 copy-start.3
  5.0 0.7 %copy-done.3 = f32[384]{0:T(512)S(1)} copy-done((f32[384]{0:T(512)S(1)}, f32[384]{0:T(512)}, u32[]{:S(2)}) %copy-start.3) | copy-done | bytes 1560
  5.7 0.0 copy-start.4
  5.7 0.7 %copy-done.4 = s32[4]{0:T(128)S(1)} copy-done((s32[4]{0:T(128)S(1)}, s32[4]{0:T(128)}, u32[]{:S(2)}) %copy-start.4) | copy-done | bytes 40
  6.3 0.0 copy-start.5
  6.3 0.7 %copy-done.5 = s32[1,4]{1,0:T(1,128)S(1)} copy-done((s32[1,4]{1,0:T(1,128)S(1)}, s32[1,4]{1,0:T(1,128)}, u32[]{:S(2)}) %copy-start.5) | copy-done | bytes 40
  7.0 27.8 %conv.1 = bf16[2,16,24,384]{3,2,1,0:T(8,128)(2,1)S(1)} custom-call(s32[4]{0:T(128)S(1)} %copy-done.4, s32[1,4]{1,0:T(1,128)S(1)} %copy-done.5, bf16[2,16,24,384]{3,2,1,0:T(8,128)(2,1)S(1)} %bitcast.5, f32[384]{0:T(512)S(1)} %copy-done.2, f32[384]{0:T(512)S(1)} %copy-done.3, bf16[3,3456,384]{2,1,0:T(8,128)(2,1)S(1)} %bitcast.3), custom_call_target="tpu_custom_call" | custom-call | tf_op jit(solution)/shard_map/conv/pallas_call | solution.py:369
  34.8 0.8 %copy.8 = bf16[1,2,16,24,384]{4,3,2,1,0:T(8,128)(2,1)} copy(bf16[1,2,16,24,384]{4,3,2,1,0:T(8,128)(2,1)S(1)} %bitcast.4) | data formatting | bytes 1179648
Async XLA Ops:
  0.0 3.3 %copy-start = (bf16[3,3,3,384,384]{4,3,2,1,0:T(8,128)(2,1)S(1)}, bf16[3,3,3,384,384]{4,3,2,1,0:T(8,128)(2,1)}, u32[]{:S(2)}) copy-start(bf16[3,3,3,384,384]{4,3,2,1,0:T(8,128)(2,1)} %param.10) | copy-start | bytes 23887876
  3.3 1.1 %copy-start.1 = (bf16[1,2,16,24,384]{4,3,2,1,0:T(8,128)(2,1)S(1)}, bf16[1,2,16,24,384]{4,3,2,1,0:T(8,128)(2,1)}, u32[]{:S(2)}) copy-start(bf16[1,2,16,24,384]{4,3,2,1,0:T(8,128)(2,1)} %param.6) | copy-start | bytes 1769476
  4.3 0.7 %copy-start.2 = (f32[384]{0:T(512)S(1)}, f32[384]{0:T(512)}, u32[]{:S(2)}) copy-start(f32[384]{0:T(512)} %gain_ref.1) | copy-start | bytes 4612
  5.0 0.7 %copy-start.3 = (f32[384]{0:T(512)S(1)}, f32[384]{0:T(512)}, u32[]{:S(2)}) copy-start(f32[384]{0:T(512)} %bias_ref.1) | copy-start | bytes 4612
  5.7 0.7 %copy-start.4 = (s32[4]{0:T(128)S(1)}, s32[4]{0:T(128)}, u32[]{:S(2)}) copy-start(s32[4]{0:T(128)} %slot_ref.1) | copy-start | bytes 52
  6.3 0.7 %copy-start.5 = (s32[1,4]{1,0:T(1,128)S(1)}, s32[1,4]{1,0:T(1,128)}, u32[]{:S(2)}) copy-start(s32[1,4]{1,0:T(1,128)} %margin_ref.1) | copy-start | bytes 52
where the time goes:
time: 35.9 us; the launch traced here: 35.7 us
  Pallas kernels  27.8 us (77%)
  local copies, waits for them, and re-layouts  7.81 us (22%)
    pallas_call x1, Pallas kernels, local(): pl.pallas_call(functools.partial(body, n_group, n_tile), out_shape=jax.Sh...  27.8 us
    unnamed x13, local copies, waits for them, and re-layouts  7.81 us

commit v1 on v0

--- a/solution.py
+++ b/solution.py
@@ -120,6 +120,8 @@
     for k in (0, 1):
         for h in (0, 1):
             block_pass(1, 1, k, h).start()
+    for h in (0, 1):
+        block_pass(1, 0, 0, h).start()
 
     zero_rim = jnp.zeros((pitch, 128), jnp.float32)
     for slot in range(2):
@@ -198,23 +200,22 @@
             rim_at(3, n)[f] = choose(hit, rim_at(1, n)[f], rim_at(0, n)[f]).astype(jnp.bfloat16)
         rim_pass(2, n).start()
 
-    def rims(kind, f, slot):
-        store = functools.partial(put_act, slot)
-
+    def rims(kind):
         def one(n):
             step_r, step_c = DIRS[n]
-            if kind:
-                v = choose(mine[way(n)], rim_at(1, n)[f], rim_at(2, n)[f])
-            else:
-                v = rim_at(0, n)[f]
-            v = activate(v, gain)
             vertical = (core_h + 1) * pitch if step_r > 0 else 0
-            if step_c == 0:
-                store(pl.ds(vertical + 8, core_w), v)
-            elif step_r == 0:
-                store(pl.ds(pitch + (8 + core_w if step_c > 0 else 7), core_h, stride=pitch), v)
-            else:
-                store(pl.ds(vertical + (8 + core_w if step_c > 0 else 7), 1), v[0:1] if step_c > 0 else v[7:8])
+            for f in range(frames):
+                if kind:
+                    v = choose(mine[way(n)], rim_at(1, n)[f], rim_at(2, n)[f])
+                else:
+                    v = rim_at(0, n)[f]
+                v = activate(v, gain)
+                if step_c == 0:
+                    put_act(f, pl.ds(vertical + 8, core_w), v)
+                elif step_r == 0:
+                    put_act(f, pl.ds(pitch + (8 + core_w if step_c > 0 else 7), core_h, stride=pitch), v)
+                else:
+                    put_act(f, pl.ds(vertical + (8 + core_w if step_c > 0 else 7), 1), v[0:1] if step_c > 0 else v[7:8])
         for_dirs(one)
 
     def column(kind, slot, b, p):
@@ -264,26 +265,37 @@
             out += [jnp.concatenate(near, axis=0), rows(plain, j0 + 1, j1 + 1), jnp.concatenate(far, axis=0)]
         return jnp.concatenate(out, axis=-1)
 
-    def multiply(slot, tap, target, many, j0, j1, between=None):
-        at = slice(j0 * core_h, j1 * core_h)
-        steps = many * lanes // 2 if many > 1 else lanes - 1
-        stride = 2 if many > 1 else 1
-
+    def product(slot, first, target, at, j0, j1, whole):
+        r = jnp.dot(windows(slot, j0, j1), w[:, pl.ds(pl.multiple_of(first * 128, 128), 256)],
+                    preferred_element_type=jnp.float32)
+
+        @pl.when(whole)
+        def _():
+            acc[target, at] += r[:, :128]
+        acc[target + 1, at] += r[:, 128:]
+
+    everything = slice(0, core_h * core_w)
+
+    def own_steps(q, carry):
+        ahead = jnp.maximum(q - lanes, 0)
+        first = jnp.where(q < lanes, 2 * q, ahead)
+        target = jnp.where(q < lanes, 2 * q, lanes + ahead)
+        product(jnp.where(q < lanes, 0, 1), first, target, everything, 0, core_w, ahead == 0)
+        return carry
+
+    def both_steps(n, carry):
+        product(1, lanes + 2 * n, 2 * n, everything, 0, core_w, n >= 0)
+
+        @pl.when(n == 0)
+        def _():
+            forward(0, 1)
+        return carry
+
+    def last_steps(j0, j1):
         def step(n, carry):
-            first = pl.multiple_of((tap * lanes + stride * n) * 128, 128)
-            r = jnp.dot(windows(slot, j0, j1), w[:, pl.ds(first, 256)], preferred_element_type=jnp.float32)
-            c = target * lanes + stride * n
-            if many > 1:
-                acc[c, at] += r[:, :128]
-            else:
-                @pl.when(n == 0)
-                def _():
-                    acc[c, at] += r[:, :128]
-            acc[c + 1, at] += r[:, 128:]
-            if between is not None:
-                pl.when(n == 0)(between)
+            product(0, 2 * lanes + n, n, slice(j0 * core_h, j1 * core_h), j0, j1, n == 0)
             return carry
-        lax.fori_loop(0, steps, step, 0)
+        lax.fori_loop(0, lanes - 1, step, 0)
 
     bias = bias_ref[...].reshape(1, channels)
 
@@ -304,45 +316,42 @@
     interior(0, 1, 1, 0, core_w)
     for_dirs(lambda n: rim_copy(opposite(n)).wait_recv())
     for_dirs(lambda n: rim_pass(1, n).start())
+    rims(0)
     for f in (0, 1):
-        rims(0, f, f)
         spread_all(0, f)
         forward(1, f)
     for_dirs(forward_rim)
-    for k in (0, 1):
-        for h in (0, 1):
-            block_pass(1, 0, k, h).start()
+    for h in (0, 1):
+        block_pass(1, 0, 1, h).start()
     w_copy(2).wait()
     w_copy(1).wait()
-    multiply(0, 0, 0, 2, 0, core_w)
-    multiply(1, 0, 1, 1, 0, core_w)
-
+    lax.fori_loop(0, 2 * lanes - 1, own_steps, 0)
+
+    forward(0, 0)
     for k in (0, 1):
         for h in (0, 1):
             block_pass(2, 1, k, h).wait_recv()
     interior(1, 1, 1, 0, core_w)
     for_dirs(lambda n: rim_pass(2, n).wait_recv())
-    rims(1, 1, 1)
+    rims(1)
     spread_all(1, 1)
-    forward(0, 0)
     w_copy(0).wait()
-    multiply(1, 1, 0, 2, 0, core_w, functools.partial(forward, 0, 1))
+    lax.fori_loop(0, lanes, both_steps, 0)
     give(1, 0, core_w)
 
     for h in (0, 1):
         block_pass(2, 0, 0, h).wait_recv()
     interior(1, 0, 0, 0, cut)
-    rims(1, 0, 0)
     spread(1, 0, 0, cut + 1)
     spread_left(1, 0)
-    multiply(0, 2, 0, 1, 0, cut - 1)
+    last_steps(0, cut - 1)
     give(0, 0, cut - 8)
     for h in (0, 1):
         block_pass(2, 0, 1, h).wait_recv()
     interior(1, 0, 0, cut, core_w)
     spread(1, 0, cut + 1, core_w + 2)
     spread_right(1, 0)
-    multiply(0, 2, 0, 1, cut - 1, core_w)
+    last_steps(cut - 1, core_w)
     give(0, cut - 8, core_w)
 
     def sent(n):
@@ -368,7 +377,7 @@
     anywhere = pl.BlockSpec(memory_space=pl.ANY)
     out = pl.pallas_call(
         functools.partial(body, n_group, n_tile),
-        out_shape=jax.ShapeDtypeStruct(x.shape, jnp.bfloat16),
+        out_shape=pltpu.VMEM(x.shape, jnp.bfloat16),
         in_specs=[smem, smem, anywhere, vmem, vmem, anywhere],
         out_specs=vmem,
         scratch_shapes=[
@@ -389,7 +398,7 @@
             pltpu.SemaphoreType.DMA((3,)),
             pltpu.SemaphoreType.DMA,
         ],
-        compiler_params=pltpu.CompilerParams(collective_id=0, has_side_effects=True, vmem_limit_bytes=40 << 20),
+        compiler_params=pltpu.CompilerParams(collective_id=0, has_side_effects=True, vmem_limit_bytes=60 << 20),
         name="conv",
     )(group_slot, margins, x, norm_gain, conv_bias, weights)
     return out[None]

time: 35.9 us -> 30.1 us (0.84)
  local copies, waits for them, and re-layouts: 7.81 us -> 0.82 us
  Pallas kernels: 27.8 us -> 29.2 us
    unnamed x13 -> x1, local copies, waits for them, and re-layouts: 7.81 us -> 0.82 us
    pallas_call x1, Pallas kernels: 27.8 us -> 29.2 us  [local(): pl.pallas_call(functools.partial(body, n_group, n_tile), out_shape=pltpu....]
where the time goes in v1:
time: 30.1 us; the launch traced here: 30 us
  Pallas kernels  29.2 us (97%)
  local copies, waits for them, and re-layouts  0.82 us (3%)
    pallas_call x1, Pallas kernels, local(): pl.pallas_call(functools.partial(body, n_group, n_tile), out_shape=pltpu....  29.2 us
    unnamed x1, local copies, waits for them, and re-layouts  0.82 us

profile of v1, /device:TPU:0, one launch (start us, length us, event | category | flops | bytes accessed | tf_op | source)
XLA Modules:
  0.0 30.0 jit_solution(12682491791533588182)
XLA Ops:
  0.0 29.2 %conv.1 = bf16[2,16,24,384]{3,2,1,0:T(8,128)(2,1)S(1)} custom-call(s32[4]{0:T(128)} %slot_ref.1, s32[1,4]{1,0:T(1,128)} %margin_ref.1, bf16[2,16,24,384]{3,2,1,0:T(8,128)(2,1)} %bitcast.5, f32[384]{0:T(512)} %gain_ref.1, f32[384]{0:T(512)} %bias_ref.1, bf16[3,3456,384]{2,1,0:T(8,128)(2,1)} %bitcast.4), custom_call_target="tpu_custom_call" | custom-call | tf_op jit(solution)/shard_map/conv/pallas_call | solution.py:378
  29.2 0.8 %copy.8 = bf16[1,2,16,24,384]{4,3,2,1,0:T(8,128)(2,1)} copy(bf16[1,2,16,24,384]{4,3,2,1,0:T(8,128)(2,1)S(1)} %bitcast.3) | data formatting | bytes 1179648

commit v2 on v1

--- a/solution.py
+++ b/solution.py
@@ -20,16 +20,17 @@
     return half + half * jnp.tanh(half)
 
 
-def body(n_group, n_tile, slot_ref, margin_ref, x_hbm, gain_ref, bias_ref, w_hbm, out_ref,
+def body(n_group, n_tile, slot_hbm, margin_hbm, x_hbm, gain_hbm, bias_hbm, w_hbm, out_ref,
          x_ref, first_in, second_in, relay, rows_in, cols_in, corners_in, cols_out, w, act, z, edge, acc,
-         send_small, recv_small, send_big, recv_big, w_sem, x_sem):
+         send_small, recv_small, send_big, recv_big, w_sem, x_sem,
+         slot_ref, margin_ref, gain_ref, bias_ref, small_sem):
     frames, core_h, core_w, channels = x_ref.shape
     grid_cols = n_tile // GRID_R
     lanes = channels // 128
     pitch = core_w + 16
     half = core_h // 2
     cut = core_w - 8
-    pieces = ((0, cut), (cut, core_w))
+    pieces = ((0, 8), (8, cut), (cut, core_w))
     group = lax.axis_index("group")
     tile = lax.axis_index("tile")
     tile_row = tile // grid_cols
@@ -60,6 +61,10 @@
 
     x_copy = pltpu.make_async_copy(x_hbm, x_ref, x_sem)
     x_copy.start()
+    small = [pltpu.make_async_copy(a, b, small_sem.at[k]) for k, (a, b) in enumerate(
+        ((slot_hbm, slot_ref), (margin_hbm, margin_ref), (gain_hbm, gain_ref), (bias_hbm, bias_ref)))]
+    for copy in small:
+        copy.start()
 
     def w_copy(a):
         return pltpu.make_async_copy(w_hbm.at[a], w.at[:, pl.ds((2 - a) * channels, channels)], w_sem.at[a])
@@ -104,7 +109,7 @@
         return pltpu.make_async_remote_copy(
             src_ref=(x_hbm if phase == 1 else relay).at[f, rows, cols],
             dst_ref=(first_in if phase == 1 else second_in).at[f, rows, cols],
-            send_sem=send_big.at[phase - 1, f, 2 * k + h], recv_sem=recv_big.at[phase - 1, f, 2 * k + h],
+            send_sem=send_big.at[phase - 1, f, k, h], recv_sem=recv_big.at[phase - 1, f, k, h],
             device_id={"group": partners[h if phase == 1 else 1 - h]}, device_id_type=MESH)
 
     def for_dirs(act_on, side=None):
@@ -117,11 +122,9 @@
 
     pl.semaphore_wait(barrier, greeted)
     for_dirs(lambda n: rim_copy(n).start(), False)
-    for k in (0, 1):
+    for f, k in ((1, 0), (1, 1), (1, 2), (0, 0)):
         for h in (0, 1):
-            block_pass(1, 1, k, h).start()
-    for h in (0, 1):
-        block_pass(1, 0, 0, h).start()
+            block_pass(1, f, k, h).start()
 
     zero_rim = jnp.zeros((pitch, 128), jnp.float32)
     for slot in range(2):
@@ -138,6 +141,8 @@
         cols_out[1, f] = side[:, core_w - 1, :].astype(jnp.bfloat16)
     for_dirs(lambda n: rim_copy(n).start(), True)
 
+    for copy in small:
+        copy.wait()
     gain = gain_ref[...].reshape(1, channels)
     left, right, up, down = [margin_ref[0, k] for k in range(4)]
     place = slot_ref[group]
@@ -167,8 +172,8 @@
     def interior(kind, f, slot, first, last):
         def some_rows(i, carry):
             for h in (0, 1):
-                for k in range(2):
-                    row = h * half + 2 * i + k
+                for k in range(4):
+                    row = h * half + 4 * i + k
                     if kind:
                         v = choose(mine[h], first_in[f, row, first:last], second_in[f, row, first:last])
                     else:
@@ -176,7 +181,7 @@
                     at = pl.multiple_of((row + 1) * pitch + 8 + first, 8)
                     put_act(slot, pl.ds(at, last - first), activate(v, gain))
             return carry
-        lax.fori_loop(0, half // 2, some_rows, 0)
+        lax.fori_loop(0, half // 4, some_rows, 0)
 
     def forward(f, k):
         first, last = pieces[k]
@@ -269,26 +274,46 @@
         r = jnp.dot(windows(slot, j0, j1), w[:, pl.ds(pl.multiple_of(first * 128, 128), 256)],
                     preferred_element_type=jnp.float32)
 
-        @pl.when(whole)
-        def _():
+        def left_part():
             acc[target, at] += r[:, :128]
+        if whole is None:
+            left_part()
+        else:
+            pl.when(whole)(left_part)
         acc[target + 1, at] += r[:, 128:]
 
     everything = slice(0, core_h * core_w)
 
-    def own_steps(q, carry):
-        ahead = jnp.maximum(q - lanes, 0)
-        first = jnp.where(q < lanes, 2 * q, ahead)
-        target = jnp.where(q < lanes, 2 * q, lanes + ahead)
-        product(jnp.where(q < lanes, 0, 1), first, target, everything, 0, core_w, ahead == 0)
+    def at_step(n, turn, act_on):
+        pl.when(n == turn)(act_on)
+
+    def forward_next():
+        for k in range(3):
+            forward(1, k)
+
+    def send_last():
+        for_dirs(forward_rim)
+        for k in (1, 2):
+            for h in (0, 1):
+                block_pass(1, 0, k, h).start()
+        forward(0, 0)
+
+    def forward_last():
+        for k in (1, 2):
+            forward(0, k)
+
+    def own_both(n, carry):
+        product(0, 2 * n, 2 * n, everything, 0, core_w, None)
+        at_step(n, 0, send_last)
         return carry
 
+    def own_single(n, carry):
+        product(1, n, lanes + n, everything, 0, core_w, n == 0)
+        return carry
+
     def both_steps(n, carry):
-        product(1, lanes + 2 * n, 2 * n, everything, 0, core_w, n >= 0)
-
-        @pl.when(n == 0)
-        def _():
-            forward(0, 1)
+        product(1, lanes + 2 * n, 2 * n, everything, 0, core_w, None)
+        at_step(n, 0, forward_last)
         return carry
 
     def last_steps(j0, j1):
@@ -319,19 +344,16 @@
     rims(0)
     for f in (0, 1):
         spread_all(0, f)
-        forward(1, f)
-    for_dirs(forward_rim)
-    for h in (0, 1):
-        block_pass(1, 0, 1, h).start()
+    forward_next()
     w_copy(2).wait()
     w_copy(1).wait()
-    lax.fori_loop(0, 2 * lanes - 1, own_steps, 0)
-
-    forward(0, 0)
-    for k in (0, 1):
+    lax.fori_loop(0, lanes, own_both, 0)
+    lax.fori_loop(0, lanes - 1, own_single, 0)
+
+    for k, (first, last) in enumerate(pieces):
         for h in (0, 1):
             block_pass(2, 1, k, h).wait_recv()
-    interior(1, 1, 1, 0, core_w)
+        interior(1, 1, 1, first, last)
     for_dirs(lambda n: rim_pass(2, n).wait_recv())
     rims(1)
     spread_all(1, 1)
@@ -339,20 +361,20 @@
     lax.fori_loop(0, lanes, both_steps, 0)
     give(1, 0, core_w)
 
-    for h in (0, 1):
-        block_pass(2, 0, 0, h).wait_recv()
+    for k in (0, 1):
+        for h in (0, 1):
+            block_pass(2, 0, k, h).wait_recv()
     interior(1, 0, 0, 0, cut)
     spread(1, 0, 0, cut + 1)
     spread_left(1, 0)
     last_steps(0, cut - 1)
-    give(0, 0, cut - 8)
     for h in (0, 1):
-        block_pass(2, 0, 1, h).wait_recv()
+        block_pass(2, 0, 2, h).wait_recv()
     interior(1, 0, 0, cut, core_w)
     spread(1, 0, cut + 1, core_w + 2)
     spread_right(1, 0)
     last_steps(cut - 1, core_w)
-    give(0, cut - 8, core_w)
+    give(0, 0, core_w)
 
     def sent(n):
         rim_copy(n).wait_send()
@@ -361,7 +383,7 @@
     for_dirs(sent)
     for phase in (1, 2):
         for f in (1, 0):
-            for k in (0, 1):
+            for k in range(3):
                 for h in (0, 1):
                     block_pass(phase, f, k, h).wait_send()
 
@@ -373,12 +395,11 @@
     pitch = core_w + 16
     block = pltpu.VMEM((frames, core_h, core_w, channels), jnp.bfloat16)
     vmem = pl.BlockSpec(memory_space=pltpu.VMEM)
-    smem = pl.BlockSpec(memory_space=pltpu.SMEM)
     anywhere = pl.BlockSpec(memory_space=pl.ANY)
     out = pl.pallas_call(
         functools.partial(body, n_group, n_tile),
         out_shape=pltpu.VMEM(x.shape, jnp.bfloat16),
-        in_specs=[smem, smem, anywhere, vmem, vmem, anywhere],
+        in_specs=[anywhere] * 6,
         out_specs=vmem,
         scratch_shapes=[
             block, block, block, block,
@@ -393,10 +414,15 @@
             pltpu.VMEM((2 * channels // 128, core_h * core_w, 128), jnp.float32),
             pltpu.SemaphoreType.DMA((3, 8)),
             pltpu.SemaphoreType.DMA((3, 8)),
-            pltpu.SemaphoreType.DMA((2, 2, 4)),
-            pltpu.SemaphoreType.DMA((2, 2, 4)),
+            pltpu.SemaphoreType.DMA((2, 2, 3, 2)),
+            pltpu.SemaphoreType.DMA((2, 2, 3, 2)),
             pltpu.SemaphoreType.DMA((3,)),
             pltpu.SemaphoreType.DMA,
+            pltpu.SMEM(group_slot.shape, jnp.int32),
+            pltpu.SMEM(margins.shape, jnp.int32),
+            pltpu.VMEM(norm_gain.shape, jnp.float32),
+            pltpu.VMEM(conv_bias.shape, jnp.float32),
+            pltpu.SemaphoreType.DMA((4,)),
         ],
         compiler_params=pltpu.CompilerParams(collective_id=0, has_side_effects=True, vmem_limit_bytes=60 << 20),
         name="conv",

time: 30.1 us -> 28.5 us (0.947)
  Pallas kernels: 29.2 us -> 27.5 us
    pallas_call x1, Pallas kernels: 29.2 us -> 27.5 us  [local(): pl.pallas_call(functools.partial(body, n_group, n_tile), out_shape=pltpu....]
where the time goes in v2:
time: 28.5 us; the launch traced here: 28.4 us
  Pallas kernels  27.5 us (96%)
  local copies, waits for them, and re-layouts  0.82 us (3%)
    pallas_call x1, Pallas kernels, local(): pl.pallas_call(functools.partial(body, n_group, n_tile), out_shape=pltpu....  27.5 us
    unnamed x1, local copies, waits for them, and re-layouts  0.82 us

profile of v2, /device:TPU:0, one launch (start us, length us, event | category | flops | bytes accessed | tf_op | source)
XLA Modules:
  0.0 28.4 jit_solution(11944987711646157883)
XLA Ops:
  0.0 27.5 %conv.1 = bf16[2,16,24,384]{3,2,1,0:T(8,128)(2,1)S(1)} custom-call(s32[4]{0:T(128)} %slot_hbm.1, s32[1,4]{1,0:T(1,128)} %margin_hbm.1, bf16[2,16,24,384]{3,2,1,0:T(8,128)(2,1)} %bitcast.5, f32[384]{0:T(512)} %gain_hbm.1, f32[384]{0:T(512)} %bias_hbm.1, bf16[3,3456,384]{2,1,0:T(8,128)(2,1)} %bitcast.4), custom_call_target="tpu_custom_call" | custom-call | tf_op jit(solution)/shard_map/conv/pallas_call | solution.py:399
  27.5 0.8 %copy.8 = bf16[1,2,16,24,384]{4,3,2,1,0:T(8,128)(2,1)} copy(bf16[1,2,16,24,384]{4,3,2,1,0:T(8,128)(2,1)S(1)} %bitcast.3) | data formatting | bytes 1179648

commit v3 on v2

--- a/solution.py
+++ b/solution.py
@@ -170,10 +170,12 @@
             act[slot, c, at] = v[:, c * 128:(c + 1) * 128]
 
     def interior(kind, f, slot, first, last):
+        many = half // 2 if last - first > 8 else half
+
         def some_rows(i, carry):
             for h in (0, 1):
-                for k in range(4):
-                    row = h * half + 4 * i + k
+                for k in range(many):
+                    row = h * half + many * i + k
                     if kind:
                         v = choose(mine[h], first_in[f, row, first:last], second_in[f, row, first:last])
                     else:
@@ -181,7 +183,7 @@
                     at = pl.multiple_of((row + 1) * pitch + 8 + first, 8)
                     put_act(slot, pl.ds(at, last - first), activate(v, gain))
             return carry
-        lax.fori_loop(0, half // 4, some_rows, 0)
+        lax.fori_loop(0, half // many, some_rows, 0)
 
     def forward(f, k):
         first, last = pieces[k]
@@ -235,7 +237,7 @@
             for b in range(3):
                 z[slot, b, pl.ds(pl.multiple_of(p * core_h, core_h), core_h)] = column(kind, slot, b, p).astype(jnp.bfloat16)
             return carry
-        lax.fori_loop(first, last, one_col, 0, unroll=2)
+        lax.fori_loop(first, last, one_col, 0, unroll=3)
 
     def spread_left(kind, slot):
         for j in range(M):
@@ -316,11 +318,11 @@
         at_step(n, 0, forward_last)
         return carry
 
-    def last_steps(j0, j1):
-        def step(n, carry):
-            product(0, 2 * lanes + n, n, slice(j0 * core_h, j1 * core_h), j0, j1, n == 0)
-            return carry
-        lax.fori_loop(0, lanes - 1, step, 0)
+    def static_product(slot, first, target, many, j0, j1):
+        r = jnp.dot(windows(slot, j0, j1), w[:, first * 128:(first + many) * 128],
+                    preferred_element_type=jnp.float32)
+        for c in range(many):
+            acc[target + c, j0 * core_h:j1 * core_h] += r[:, c * 128:(c + 1) * 128]
 
     bias = bias_ref[...].reshape(1, channels)
 
@@ -330,7 +332,7 @@
                                  for c in range(lanes)], axis=-1)
             out_ref[s, i, first:last] = (v + bias).astype(out_ref.dtype)
             return carry
-        lax.fori_loop(0, core_h, put, 0, unroll=4)
+        lax.fori_loop(0, core_h, put, 0, unroll=8)
 
     def clear(i, carry):
         acc[i] = jnp.zeros(acc.shape[1:], jnp.float32)
@@ -361,31 +363,32 @@
     lax.fori_loop(0, lanes, both_steps, 0)
     give(1, 0, core_w)
 
+    def sent(n):
+        rim_copy(n).wait_send()
+        for phase in (1, 2):
+            rim_pass(phase, n).wait_send()
+    for_dirs(sent)
+    for phase, f in ((1, 1), (2, 1), (1, 0)):
+        for k in range(3):
+            for h in (0, 1):
+                block_pass(phase, f, k, h).wait_send()
+
     for k in (0, 1):
         for h in (0, 1):
             block_pass(2, 0, k, h).wait_recv()
-    interior(1, 0, 0, 0, cut)
+        interior(1, 0, 0, *pieces[k])
     spread(1, 0, 0, cut + 1)
     spread_left(1, 0)
-    last_steps(0, cut - 1)
     for h in (0, 1):
         block_pass(2, 0, 2, h).wait_recv()
     interior(1, 0, 0, cut, core_w)
     spread(1, 0, cut + 1, core_w + 2)
     spread_right(1, 0)
-    last_steps(cut - 1, core_w)
+    static_product(0, 2 * lanes, 0, lanes, 0, core_w)
     give(0, 0, core_w)
-
-    def sent(n):
-        rim_copy(n).wait_send()
-        for phase in (1, 2):
-            rim_pass(phase, n).wait_send()
-    for_dirs(sent)
-    for phase in (1, 2):
-        for f in (1, 0):
-            for k in range(3):
-                for h in (0, 1):
-                    block_pass(phase, f, k, h).wait_send()
+    for k in range(3):
+        for h in (0, 1):
+            block_pass(2, 0, k, h).wait_send()
 
 
 def local(n_group, n_tile, features, group_slot, margins, norm_gain, kernel, conv_bias):

time: 28.5 us -> 27.2 us (0.954)
  Pallas kernels: 27.5 us -> 26.2 us
    pallas_call x1, Pallas kernels: 27.5 us -> 26.2 us  [local(): pl.pallas_call(functools.partial(body, n_group, n_tile), out_shape=pltpu....]
where the time goes in v3:
time: 27.2 us; the launch traced here: 27 us
  Pallas kernels  26.2 us (96%)
  local copies, waits for them, and re-layouts  0.82 us (3%)
    pallas_call x1, Pallas kernels, local(): pl.pallas_call(functools.partial(body, n_group, n_tile), out_shape=pltpu....  26.2 us
    unnamed x1, local copies, waits for them, and re-layouts  0.82 us

profile of v3, /device:TPU:0, one launch (start us, length us, event | category | flops | bytes accessed | tf_op | source)
XLA Modules:
  0.0 27.0 jit_solution(7632293021465869723)
XLA Ops:
  0.0 26.2 %conv.1 = bf16[2,16,24,384]{3,2,1,0:T(8,128)(2,1)S(1)} custom-call(s32[4]{0:T(128)} %slot_hbm.1, s32[1,4]{1,0:T(1,128)} %margin_hbm.1, bf16[2,16,24,384]{3,2,1,0:T(8,128)(2,1)} %bitcast.5, f32[384]{0:T(512)} %gain_hbm.1, f32[384]{0:T(512)} %bias_hbm.1, bf16[3,3456,384]{2,1,0:T(8,128)(2,1)} %bitcast.4), custom_call_target="tpu_custom_call" | custom-call | tf_op jit(solution)/shard_map/conv/pallas_call | solution.py:402
  26.2 0.8 %copy.8 = bf16[1,2,16,24,384]{4,3,2,1,0:T(8,128)(2,1)} copy(bf16[1,2,16,24,384]{4,3,2,1,0:T(8,128)(2,1)S(1)} %bitcast.3) | data formatting | bytes 1179648

commit v4 on v3

--- a/solution.py
+++ b/solution.py
@@ -315,7 +315,7 @@
 
     def both_steps(n, carry):
         product(1, lanes + 2 * n, 2 * n, everything, 0, core_w, None)
-        at_step(n, 0, forward_last)
+        at_step(n, 0, functools.partial(forward, 0, 2))
         return carry
 
     def static_product(slot, first, target, many, j0, j1):
@@ -346,7 +346,8 @@
     rims(0)
     for f in (0, 1):
         spread_all(0, f)
-    forward_next()
+        forward(1, f)
+    forward(1, 2)
     w_copy(2).wait()
     w_copy(1).wait()
     lax.fori_loop(0, lanes, own_both, 0)
@@ -360,6 +361,7 @@
     rims(1)
     spread_all(1, 1)
     w_copy(0).wait()
+    forward(0, 1)
     lax.fori_loop(0, lanes, both_steps, 0)
     give(1, 0, core_w)
 

time: 27.2 us -> 27 us (level)
  no operation moved by 1% of the time
where the time goes in v4:
time: 27 us; the launch traced here: 26.8 us
  Pallas kernels  26 us (96%)
  local copies, waits for them, and re-layouts  0.82 us (3%)
    pallas_call x1, Pallas kernels, local(): pl.pallas_call(functools.partial(body, n_group, n_tile), out_shape=pltpu....  26 us
    unnamed x1, local copies, waits for them, and re-layouts  0.82 us

profile of v4, /device:TPU:0, one launch (start us, length us, event | category | flops | bytes accessed | tf_op | source)
XLA Modules:
  0.0 26.8 jit_solution(13937659125927276209)
XLA Ops:
  0.0 26.0 %conv.1 = bf16[2,16,24,384]{3,2,1,0:T(8,128)(2,1)S(1)} custom-call(s32[4]{0:T(128)} %slot_hbm.1, s32[1,4]{1,0:T(1,128)} %margin_hbm.1, bf16[2,16,24,384]{3,2,1,0:T(8,128)(2,1)} %bitcast.5, f32[384]{0:T(512)} %gain_hbm.1, f32[384]{0:T(512)} %bias_hbm.1, bf16[3,3456,384]{2,1,0:T(8,128)(2,1)} %bitcast.4), custom_call_target="tpu_custom_call" | custom-call | tf_op jit(solution)/shard_map/conv/pallas_call | solution.py:404
  26.0 0.8 %copy.8 = bf16[1,2,16,24,384]{4,3,2,1,0:T(8,128)(2,1)} copy(bf16[1,2,16,24,384]{4,3,2,1,0:T(8,128)(2,1)S(1)} %bitcast.3) | data formatting | bytes 1179648
